TPU v7x, 512 devices: a whole 4x8x8 slice. The times are simulated.
512 devices in a mesh: section: 16 (over x_hi, y), fsdp: 32 (over x_lo, z, core).
Axes of the slice: x: 4 (x_hi: 2, x_lo: 2; x = x_hi * 2 + x_lo), y: 8, z: 8, core: 2. Of those that a mesh axis runs over, the one named last changes fastest.
Arguments:
- inputs: bfloat16 [16, 8, 1024, 4096], P('section', None, 'fsdp'), may hold values from -6 to 6
- upstream: bfloat16 [8, 1024, 4096], P(None, 'fsdp'), may hold values from -6 to 6
- weights: bfloat16 [16, 4096, 512], P('section', 'fsdp')
- gain: bfloat16 [16, 4096], P('section', 'fsdp'), may hold values from 0.5 to 1.5
Outputs:
- weight_grad: float32 [16, 4096, 512], P('section', 'fsdp')
- gain_grad: float32 [16, 4096], P('section')
All inputs are finite; a program needn't handle non-finite values.
Results may differ from a plain program's by a relative error of at most 0.035.
Values may be sent and summed in bfloat16 or wider, within the bound.
No kernel may reach another device: no remote copies, remote signals or barrier semaphores. Data moves between devices by JAX's collectives and lax.ppermute only.
A program may use at most 128 MiB of HBM per device.

v0:
```python
import jax
import jax.numpy as jnp
from jax import lax
from jax.sharding import PartitionSpec as P


def passed_along(value, axis, steps):
    count = lax.axis_size(axis)
    leading, last = (max(0, -steps), min(count, count - steps))
    return lax.ppermute(value, axis, [(source, source + steps) for source in range(leading, last)])


def rope_tables(length, head):
    half_head = head // 2
    position = lax.iota(jnp.float32, length)
    freq = jnp.power(500000.0, -2.0 * lax.iota(jnp.float32, half_head) / head)
    angle = position[:, None] * freq[None, :]
    return (jnp.cos(angle), jnp.sin(angle))


def rotate(value_rows, cosine, sine_table):
    half_head = value_rows.shape[-1] // 2
    first = value_rows[..., :half_head]
    second = value_rows[..., half_head:]
    return jnp.concatenate(
        [first * cosine - second * sine_table, second * cosine + first * sine_table], axis=-1
    )


def unrotate(value_rows, cosine, sine_table):
    half_head = value_rows.shape[-1] // 2
    first = value_rows[..., :half_head]
    second = value_rows[..., half_head:]
    return jnp.concatenate(
        [first * cosine + second * sine_table, second * cosine - first * sine_table], axis=-1
    )


def contract_rows(left, right):
    return lax.dot_general(
        left, right, (((0,), (0,)), ((), ())), preferred_element_type=jnp.float32
    )


def contract_cols(left, right):
    return lax.dot_general(
        left, right, (((1,), (1,)), ((), ())), preferred_element_type=jnp.float32
    )


def on_device(inputs, upstream, weights, gain):
    sections = lax.axis_size("section")
    here = lax.axis_index("section")
    micro_count = inputs.shape[1]
    length = inputs.shape[2]
    width = inputs.shape[3]
    head = weights.shape[2] // 4
    tokens_all = micro_count * length
    xfloat = inputs[0].reshape(tokens_all, width).astype(jnp.float32)
    inv_rms = lax.rsqrt(jnp.mean(xfloat * xfloat, axis=1, keepdims=True) + 1e-05)
    normed = xfloat * inv_rms
    w_full, gain_full = (
        lax.all_gather(weights[0], "fsdp", axis=0, tiled=True),
        lax.all_gather(gain[0], "fsdp", axis=0, tiled=True),
    )
    hidden = (normed * gain_full.astype(jnp.float32)).astype(jnp.bfloat16)
    proj = jnp.dot(hidden, w_full[:, : 3 * head], preferred_element_type=jnp.float32)
    wide_gain = gain_full.astype(jnp.float32)
    w_proj = w_full[:, : 3 * head]
    w_back = w_full[:, 3 * head :]
    cosine, sine_table = rope_tables(length, head)
    proj_seq = proj.reshape(micro_count, length, 3 * head)
    query_rows = rotate(proj_seq[..., :head], cosine, sine_table).astype(jnp.bfloat16)
    key_rows = rotate(proj_seq[..., head : 2 * head], cosine, sine_table).astype(jnp.bfloat16)
    value_rows = proj_seq[..., 2 * head :].astype(jnp.bfloat16)
    score_scale = head ** (-0.5)
    causal = lax.broadcasted_iota(jnp.int32, (length, length), 0) >= lax.broadcasted_iota(
        jnp.int32, (length, length), 1
    )

    def work(micro, grad_in, state):
        grad_store, proj_store, att_store, gain_acc, extra = state
        query_m = lax.dynamic_index_in_dim(query_rows, micro, 0, keepdims=False)
        keys_m = lax.dynamic_index_in_dim(key_rows, micro, 0, keepdims=False)
        values_m = lax.dynamic_index_in_dim(value_rows, micro, 0, keepdims=False)
        normed_m = lax.dynamic_slice_in_dim(normed, micro * length, length, 0)
        inv_m = lax.dynamic_slice_in_dim(inv_rms, micro * length, length, 0)
        score_matrix = contract_cols(query_m, keys_m) * score_scale
        probs = jax.nn.softmax(jnp.where(causal, score_matrix, -1e30), axis=-1)
        probability_matrix = probs.astype(jnp.bfloat16)
        attended_output = jnp.dot(
            probability_matrix, values_m, preferred_element_type=jnp.float32
        ).astype(jnp.bfloat16)
        attention_gradient = jnp.dot(grad_in, w_back, preferred_element_type=jnp.float32).astype(
            jnp.bfloat16
        )
        probability_gradient = contract_cols(attention_gradient, values_m)
        score_gradient = (
            probs
            * (probability_gradient - jnp.sum(probability_gradient * probs, axis=-1, keepdims=True))
            * score_scale
        ).astype(jnp.bfloat16)
        query_gradient = jnp.dot(score_gradient, keys_m, preferred_element_type=jnp.float32)
        key_gradient = contract_rows(score_gradient, query_m)
        value_gradient = contract_rows(probability_matrix, attention_gradient)
        grad_proj = jnp.concatenate(
            [
                unrotate(query_gradient, cosine, sine_table),
                unrotate(key_gradient, cosine, sine_table),
                value_gradient,
            ],
            axis=-1,
        ).astype(jnp.bfloat16)
        grad_hidden = contract_cols(grad_proj, w_proj)
        gain_term = jnp.sum(grad_hidden * normed_m, axis=0)
        grad_normed = grad_hidden * wide_gain
        grad_x = inv_m * (
            grad_normed - normed_m * jnp.mean(grad_normed * normed_m, axis=-1, keepdims=True)
        )
        grad_out = (grad_in.astype(jnp.float32) + grad_x).astype(jnp.bfloat16)
        grad_store = lax.dynamic_update_index_in_dim(grad_store, grad_in, micro, 0)
        proj_store = lax.dynamic_update_index_in_dim(proj_store, grad_proj, micro, 0)
        att_store = lax.dynamic_update_index_in_dim(att_store, attended_output, micro, 0)
        return (grad_out, (grad_store, proj_store, att_store, gain_acc + gain_term, extra))

    def spare(micro, grad_in, state):
        return (jnp.zeros_like(grad_in), state)

    def tick(tick_no, received, state):
        micro = tick_no - (sections - 1 - here)
        active = jnp.logical_and(micro >= 0, micro < micro_count)
        clipped = jnp.clip(micro, 0, micro_count - 1)
        top_grad = lax.dynamic_index_in_dim(upstream, clipped, 0, keepdims=False)
        grad_in = jnp.where(here == sections - 1, top_grad, received)
        return lax.cond(active, work, spare, clipped, grad_in, state)

    def step_loop(tick_no, carry):
        received, state = carry
        sent, state = tick(tick_no, received, state)
        received = passed_along(sent, "section", -1)
        return (received, state)

    extra_start = jnp.zeros((1,), jnp.float32)
    state_start = (
        jnp.zeros((micro_count, length, width), jnp.bfloat16),
        jnp.zeros((micro_count, length, 3 * head), jnp.bfloat16),
        jnp.zeros((micro_count, length, head), jnp.bfloat16),
        jnp.zeros((width,), jnp.float32),
        extra_start,
    )
    total_ticks = sections + micro_count - 1
    received, state = lax.fori_loop(
        0, total_ticks - 1, step_loop, (jnp.zeros((length, width), jnp.bfloat16), state_start)
    )
    leftover, state = tick(total_ticks - 1, received, state)
    grad_store, proj_store, att_store, gain_acc, extra = state
    gain_sum = lax.psum(gain_acc, "fsdp")
    grad_flat = grad_store.reshape(tokens_all, width)
    proj_flat = proj_store.reshape(tokens_all, 3 * head)
    att_flat = att_store.reshape(tokens_all, head)
    shard = lax.psum_scatter(
        jnp.concatenate(
            [contract_rows(hidden, proj_flat), contract_rows(grad_flat, att_flat)], axis=1
        ).astype(jnp.bfloat16),
        "fsdp",
        scatter_dimension=0,
        tiled=True,
    ).astype(jnp.float32)
    return (shard[None], gain_sum[None])


def solution(mesh):
    return jax.shard_map(
        on_device,
        mesh=mesh,
        in_specs=(
            P("section", None, "fsdp", None),
            P(None, "fsdp", None),
            P("section", "fsdp", None),
            P("section", "fsdp"),
        ),
        out_specs=(P("section", "fsdp", None), P("section", None)),
        check_vma=False,
    )
```

profile of v0, /device:TPU:8, one launch (start us, length us, event | category | flops | bytes accessed | tf_op | source)
XLA Modules:
  0.0 769.8 jit_solution(6606745490900244712)
XLA Ops:
  10.7 40.3 %all-gather = bf16[1,4096]{1,0:T(2,128)(2,1)S(1)} all-gather(bf16[1,128]{1,0:T(2,128)(2,1)} %param.13), channel_id=2, replica_groups=mesh['section'=16,'fsdp'=32] {'fsdp'}, dimensions={1}, use_global_device_ids=true | all-gather | bytes 8448 | tf_op jit(solution)/shard_map/all_gather | solution.py:64
  55.6 29.3 %all-gather.4.cloned.1.call-done = bf16[1,4096,512]{2,1,0:T(8,128)(2,1)} async-done(((bf16[1,128,512]{2,1,0:T(8,128)(2,1)}), bf16[1,4096,512]{2,1,0:T(8,128)(2,1)}) %all-gather.4.cloned.1.call-update) | async-done | bytes 4194320 | tf_op jit(solution)/shard_map/all_gather | solution.py:63
  94.9 523.2 %while.26 = (s32[]{:T(128)}, bf16[32,4096]{1,0:T(8,128)(2,1)}, bf16[8,32,4096]{2,1,0:T(8,128)(2,1)}, bf16[8,32,384]{2,1,0:T(8,128)(2,1)}, bf16[8,32,128]{2,1,0:T...) while((s32[]{:T(128)}, bf16[32,4096]{1,0:T(8,128)(2,1)}, ...), condition=%wide.region_9.10_spmd.clone.clone.clone, body=%wide.region_1.9_spmd.clone.clone.clone.sunk | while | flops 137564064 | bytes 10755985 | solution.py:152
  98.3 8.0 %collective-permute-done = bf16[32,4096]{1,0:T(8,128)(2,1)S(1)} collective-permute-done((bf16[32,4096]{1,0:T(8,128)(2,1)}, bf16[32,4096]{1,0:T(8,128)(2,1)S(1)}, u32[]{:S(2)}, u32[]{:S(2)}) %collective-permute-start) | collective-permute-done | bytes 262176 | tf_op jit(solution)/shard_map/while/body/eval_jaxpr/ppermute | solution.py:10
  121.5 7.2 collective-permute-done
  142.7 7.5 collective-permute-done
  153.6 7.8 %collective-permute-done = bf16[32,4096]{1,0:T(8,128)(2,1)S(1)} collective-permute-done((bf16[32,4096]{1,0:T(8,128)(2,1)}, bf16[32,4096]{1,0:T(8,128)(2,1)S(1)}, u32[]{:S(2)}, u32[]{:S(2)}) %collective-permute-start) | collective-permute-done | bytes 262176 | tf_op jit(solution)/shard_map/while/body/eval_jaxpr/ppermute | solution.py:10
  164.8 7.8 %collective-permute-done = bf16[32,4096]{1,0:T(8,128)(2,1)S(1)} collective-permute-done((bf16[32,4096]{1,0:T(8,128)(2,1)}, bf16[32,4096]{1,0:T(8,128)(2,1)S(1)}, u32[]{:S(2)}, u32[]{:S(2)}) %collective-permute-start) | collective-permute-done | bytes 262176 | tf_op jit(solution)/shard_map/while/body/eval_jaxpr/ppermute | solution.py:10
  175.9 7.9 %collective-permute-done = bf16[32,4096]{1,0:T(8,128)(2,1)S(1)} collective-permute-done((bf16[32,4096]{1,0:T(8,128)(2,1)}, bf16[32,4096]{1,0:T(8,128)(2,1)S(1)}, u32[]{:S(2)}, u32[]{:S(2)}) %collective-permute-start) | collective-permute-done | bytes 262176 | tf_op jit(solution)/shard_map/while/body/eval_jaxpr/ppermute | solution.py:10
  187.3 7.6 collective-permute-done
  198.3 8.9 %collective-permute-done = bf16[32,4096]{1,0:T(8,128)(2,1)S(1)} collective-permute-done((bf16[32,4096]{1,0:T(8,128)(2,1)}, bf16[32,4096]{1,0:T(8,128)(2,1)S(1)}, u32[]{:S(2)}, u32[]{:S(2)}) %collective-permute-start) | collective-permute-done | bytes 262176 | tf_op jit(solution)/shard_map/while/body/eval_jaxpr/ppermute | solution.py:10
  210.6 10.2 %collective-permute-done = bf16[32,4096]{1,0:T(8,128)(2,1)S(1)} collective-permute-done((bf16[32,4096]{1,0:T(8,128)(2,1)}, bf16[32,4096]{1,0:T(8,128)(2,1)S(1)}, u32[]{:S(2)}, u32[]{:S(2)}) %collective-permute-start) | collective-permute-done | bytes 262176 | tf_op jit(solution)/shard_map/while/body/eval_jaxpr/ppermute | solution.py:10
  224.2 11.6 %collective-permute-done = bf16[32,4096]{1,0:T(8,128)(2,1)S(1)} collective-permute-done((bf16[32,4096]{1,0:T(8,128)(2,1)}, bf16[32,4096]{1,0:T(8,128)(2,1)S(1)}, u32[]{:S(2)}, u32[]{:S(2)}) %collective-permute-start) | collective-permute-done | bytes 262176 | tf_op jit(solution)/shard_map/while/body/eval_jaxpr/ppermute | solution.py:10
  239.3 8.6 %collective-permute-done = bf16[32,4096]{1,0:T(8,128)(2,1)S(1)} collective-permute-done((bf16[32,4096]{1,0:T(8,128)(2,1)}, bf16[32,4096]{1,0:T(8,128)(2,1)S(1)}, u32[]{:S(2)}, u32[]{:S(2)}) %collective-permute-start) | collective-permute-done | bytes 262176 | tf_op jit(solution)/shard_map/while/body/eval_jaxpr/ppermute | solution.py:10
  251.3 158.1 %collective-permute-done = bf16[32,4096]{1,0:T(8,128)(2,1)S(1)} collective-permute-done((bf16[32,4096]{1,0:T(8,128)(2,1)}, bf16[32,4096]{1,0:T(8,128)(2,1)S(1)}, u32[]{:S(2)}, u32[]{:S(2)}) %collective-permute-start) | collective-permute-done | bytes 262176 | tf_op jit(solution)/shard_map/while/body/eval_jaxpr/ppermute | solution.py:10
  410.1 13.6 %conditional.7 = (bf16[32,4096]{1,0:T(8,128)(2,1)}, bf16[8,32,4096]{2,1,0:T(8,128)(2,1)}, bf16[8,32,384]{2,1,0:T(8,128)(2,1)}, bf16[8,32,128]{2,1,0:T(8,128)(2,1)}, f32[4096]{0:T(1024)S(1)}) conditional(s32[]{:T(128)} %convert_element_type.189, (bf16[8,32,4096]{2,1,0:T(8,128)(2,1)}, bf16[8,32,384]{2,1,0:T(8,128)(2,1)}, ...), branch_computations={%region_2.2_spmd, %region_3.8_spmd.clone} | conditional | flops 137562016 | bytes 8641706 | solution.py:135
  425.6 10.3 %collective-permute-done = bf16[32,4096]{1,0:T(8,128)(2,1)S(1)} collective-permute-done((bf16[32,4096]{1,0:T(8,128)(2,1)}, bf16[32,4096]{1,0:T(8,128)(2,1)S(1)}, u32[]{:S(2)}, u32[]{:S(2)}) %collective-permute-start) | collective-permute-done | bytes 262176 | tf_op jit(solution)/shard_map/while/body/eval_jaxpr/ppermute | solution.py:10
  436.6 13.6 %conditional.7 = (bf16[32,4096]{1,0:T(8,128)(2,1)}, bf16[8,32,4096]{2,1,0:T(8,128)(2,1)}, bf16[8,32,384]{2,1,0:T(8,128)(2,1)}, bf16[8,32,128]{2,1,0:T(8,128)(2,1)}, f32[4096]{0:T(1024)S(1)}) conditional(s32[]{:T(128)} %convert_element_type.189, (bf16[8,32,4096]{2,1,0:T(8,128)(2,1)}, bf16[8,32,384]{2,1,0:T(8,128)(2,1)}, ...), branch_computations={%region_2.2_spmd, %region_3.8_spmd.clone} | conditional | flops 137562016 | bytes 8641706 | solution.py:135
  452.1 10.2 %collective-permute-done = bf16[32,4096]{1,0:T(8,128)(2,1)S(1)} collective-permute-done((bf16[32,4096]{1,0:T(8,128)(2,1)}, bf16[32,4096]{1,0:T(8,128)(2,1)S(1)}, u32[]{:S(2)}, u32[]{:S(2)}) %collective-permute-start) | collective-permute-done | bytes 262176 | tf_op jit(solution)/shard_map/while/body/eval_jaxpr/ppermute | solution.py:10
  463.0 13.6 %conditional.7 = (bf16[32,4096]{1,0:T(8,128)(2,1)}, bf16[8,32,4096]{2,1,0:T(8,128)(2,1)}, bf16[8,32,384]{2,1,0:T(8,128)(2,1)}, bf16[8,32,128]{2,1,0:T(8,128)(2,1)}, f32[4096]{0:T(1024)S(1)}) conditional(s32[]{:T(128)} %convert_element_type.189, (bf16[8,32,4096]{2,1,0:T(8,128)(2,1)}, bf16[8,32,384]{2,1,0:T(8,128)(2,1)}, ...), branch_computations={%region_2.2_spmd, %region_3.8_spmd.clone} | conditional | flops 137562016 | bytes 8641706 | solution.py:135
  478.6 10.4 %collective-permute-done = bf16[32,4096]{1,0:T(8,128)(2,1)S(1)} collective-permute-done((bf16[32,4096]{1,0:T(8,128)(2,1)}, bf16[32,4096]{1,0:T(8,128)(2,1)S(1)}, u32[]{:S(2)}, u32[]{:S(2)}) %collective-permute-start) | collective-permute-done | bytes 262176 | tf_op jit(solution)/shard_map/while/body/eval_jaxpr/ppermute | solution.py:10
  489.7 13.6 %conditional.7 = (bf16[32,4096]{1,0:T(8,128)(2,1)}, bf16[8,32,4096]{2,1,0:T(8,128)(2,1)}, bf16[8,32,384]{2,1,0:T(8,128)(2,1)}, bf16[8,32,128]{2,1,0:T(8,128)(2,1)}, f32[4096]{0:T(1024)S(1)}) conditional(s32[]{:T(128)} %convert_element_type.189, (bf16[8,32,4096]{2,1,0:T(8,128)(2,1)}, bf16[8,32,384]{2,1,0:T(8,128)(2,1)}, ...), branch_computations={%region_2.2_spmd, %region_3.8_spmd.clone} | conditional | flops 137562016 | bytes 8641706 | solution.py:135
  505.2 10.0 %collective-permute-done = bf16[32,4096]{1,0:T(8,128)(2,1)S(1)} collective-permute-done((bf16[32,4096]{1,0:T(8,128)(2,1)}, bf16[32,4096]{1,0:T(8,128)(2,1)S(1)}, u32[]{:S(2)}, u32[]{:S(2)}) %collective-permute-start) | collective-permute-done | bytes 262176 | tf_op jit(solution)/shard_map/while/body/eval_jaxpr/ppermute | solution.py:10
  515.9 13.6 %conditional.7 = (bf16[32,4096]{1,0:T(8,128)(2,1)}, bf16[8,32,4096]{2,1,0:T(8,128)(2,1)}, bf16[8,32,384]{2,1,0:T(8,128)(2,1)}, bf16[8,32,128]{2,1,0:T(8,128)(2,1)}, f32[4096]{0:T(1024)S(1)}) conditional(s32[]{:T(128)} %convert_element_type.189, (bf16[8,32,4096]{2,1,0:T(8,128)(2,1)}, bf16[8,32,384]{2,1,0:T(8,128)(2,1)}, ...), branch_computations={%region_2.2_spmd, %region_3.8_spmd.clone} | conditional | flops 137562016 | bytes 8641706 | solution.py:135
  531.5 10.2 %collective-permute-done = bf16[32,4096]{1,0:T(8,128)(2,1)S(1)} collective-permute-done((bf16[32,4096]{1,0:T(8,128)(2,1)}, bf16[32,4096]{1,0:T(8,128)(2,1)S(1)}, u32[]{:S(2)}, u32[]{:S(2)}) %collective-permute-start) | collective-permute-done | bytes 262176 | tf_op jit(solution)/shard_map/while/body/eval_jaxpr/ppermute | solution.py:10
  542.5 13.6 %conditional.7 = (bf16[32,4096]{1,0:T(8,128)(2,1)}, bf16[8,32,4096]{2,1,0:T(8,128)(2,1)}, bf16[8,32,384]{2,1,0:T(8,128)(2,1)}, bf16[8,32,128]{2,1,0:T(8,128)(2,1)}, f32[4096]{0:T(1024)S(1)}) conditional(s32[]{:T(128)} %convert_element_type.189, (bf16[8,32,4096]{2,1,0:T(8,128)(2,1)}, bf16[8,32,384]{2,1,0:T(8,128)(2,1)}, ...), branch_computations={%region_2.2_spmd, %region_3.8_spmd.clone} | conditional | flops 137562016 | bytes 8641706 | solution.py:135
  558.0 10.1 %collective-permute-done = bf16[32,4096]{1,0:T(8,128)(2,1)S(1)} collective-permute-done((bf16[32,4096]{1,0:T(8,128)(2,1)}, bf16[32,4096]{1,0:T(8,128)(2,1)S(1)}, u32[]{:S(2)}, u32[]{:S(2)}) %collective-permute-start) | collective-permute-done | bytes 262176 | tf_op jit(solution)/shard_map/while/body/eval_jaxpr/ppermute | solution.py:10
  568.8 13.6 %conditional.7 = (bf16[32,4096]{1,0:T(8,128)(2,1)}, bf16[8,32,4096]{2,1,0:T(8,128)(2,1)}, bf16[8,32,384]{2,1,0:T(8,128)(2,1)}, bf16[8,32,128]{2,1,0:T(8,128)(2,1)}, f32[4096]{0:T(1024)S(1)}) conditional(s32[]{:T(128)} %convert_element_type.189, (bf16[8,32,4096]{2,1,0:T(8,128)(2,1)}, bf16[8,32,384]{2,1,0:T(8,128)(2,1)}, ...), branch_computations={%region_2.2_spmd, %region_3.8_spmd.clone} | conditional | flops 137562016 | bytes 8641706 | solution.py:135
  584.3 10.2 %collective-permute-done = bf16[32,4096]{1,0:T(8,128)(2,1)S(1)} collective-permute-done((bf16[32,4096]{1,0:T(8,128)(2,1)}, bf16[32,4096]{1,0:T(8,128)(2,1)S(1)}, u32[]{:S(2)}, u32[]{:S(2)}) %collective-permute-start) | collective-permute-done | bytes 262176 | tf_op jit(solution)/shard_map/while/body/eval_jaxpr/ppermute | solution.py:10
  595.3 13.6 %conditional.7 = (bf16[32,4096]{1,0:T(8,128)(2,1)}, bf16[8,32,4096]{2,1,0:T(8,128)(2,1)}, bf16[8,32,384]{2,1,0:T(8,128)(2,1)}, bf16[8,32,128]{2,1,0:T(8,128)(2,1)}, f32[4096]{0:T(1024)S(1)}) conditional(s32[]{:T(128)} %convert_element_type.189, (bf16[8,32,4096]{2,1,0:T(8,128)(2,1)}, bf16[8,32,384]{2,1,0:T(8,128)(2,1)}, ...), branch_computations={%region_2.2_spmd, %region_3.8_spmd.clone} | conditional | flops 137562016 | bytes 8641706 | solution.py:135
  631.0 104.5 %psum.7 = f32[1,4096]{1,0:T(1,128)} all-reduce(f32[1,4096]{1,0:T(1,128)S(1)} %bitcast.142), channel_id=1, replica_groups=mesh['section'=16,'fsdp'=32] {'fsdp'}, use_global_device_ids=true, to_apply=%region_17.18 | all-reduce | flops 4096 | bytes 32768 | tf_op jit(solution)/shard_map/psum | solution.py:157
  735.4 25.7 %reduce-scatter.4.cloned.1.call-done = bf16[128,512]{1,0:T(8,128)(2,1)} async-done(((bf16[4096,512]{1,0:T(8,128)(2,1)}), bf16[128,512]{1,0:T(8,128)(2,1)}) %reduce-scatter.4.cloned.1.call-update) | async-done | bytes 131088
  (375 shorter events, 242.1 us)
Async XLA Ops:
  7.2 44.0 %copy-start = (bf16[1,8,32,4096]{3,2,1,0:T(8,128)(2,1)S(1)}, bf16[1,8,32,4096]{3,2,1,0:T(8,128)(2,1)}, u32[]{:S(2)}) copy-start(bf16[1,8,32,4096]{3,2,1,0:T(8,128)(2,1)} %param.10) | copy-start | bytes 6291460
  7.2 77.8 %all-gather.4.cloned.1.call-start = ((), (), s32[]{:S(2)}) async-start(), calls=%async_computation.1 | async-start | bytes 4325376 | tf_op jit(solution)/shard_map/all_gather | solution.py:63
  7.9 753.2 %reduce-scatter.4.cloned.1.call-start = ((), (), s32[]{:S(2)}) async-start(), calls=%async_computation.2 | async-start | bytes 4325376
  51.1 39.3 %copy-start.5 = (f32[32,64]{1,0:T(8,128)}, f32[32,64]{1,0:T(8,128)S(1)}, u32[]{:S(2)}) copy-start(f32[32,64]{1,0:T(8,128)S(1)} %get-tuple-element.1389) | copy-start | bytes 24580
  51.1 39.3 %copy-start.6 = (f32[32,64]{1,0:T(8,128)}, f32[32,64]{1,0:T(8,128)S(1)}, u32[]{:S(2)}) copy-start(f32[32,64]{1,0:T(8,128)S(1)} %get-tuple-element.1390) | copy-start | bytes 24580
  95.7 10.5 %collective-permute-start = (bf16[32,4096]{1,0:T(8,128)(2,1)}, bf16[32,4096]{1,0:T(8,128)(2,1)S(1)}, u32[]{:S(2)}, u32[]{:S(2)}) collective-permute-start(bf16[32,4096]{1,0:T(8,128)(2,1)} %get-tuple-element.1282), channel_id=1, source_target_pairs={{32,0},{64,32},{96,64},{128,96},{160,128},{192,160},{224,192},{256... | collective-permute-start | bytes 786440 | tf_op jit(solution)/shard_map/while/body/eval_jaxpr/ppermute | solution.py:10
  107.7 9.7 %collective-permute-start = (bf16[32,4096]{1,0:T(8,128)(2,1)}, bf16[32,4096]{1,0:T(8,128)(2,1)S(1)}, u32[]{:S(2)}, u32[]{:S(2)}) collective-permute-start(bf16[32,4096]{1,0:T(8,128)(2,1)} %get-tuple-element.1282), channel_id=1, source_target_pairs={{32,0},{64,32},{96,64},{128,96},{160,128},{192,160},{224,192},{256... | collective-permute-start | bytes 786440 | tf_op jit(solution)/shard_map/while/body/eval_jaxpr/ppermute | solution.py:10
  118.9 9.8 %collective-permute-start = (bf16[32,4096]{1,0:T(8,128)(2,1)}, bf16[32,4096]{1,0:T(8,128)(2,1)S(1)}, u32[]{:S(2)}, u32[]{:S(2)}) collective-permute-start(bf16[32,4096]{1,0:T(8,128)(2,1)} %get-tuple-element.1282), channel_id=1, source_target_pairs={{32,0},{64,32},{96,64},{128,96},{160,128},{192,160},{224,192},{256... | collective-permute-start | bytes 786440 | tf_op jit(solution)/shard_map/while/body/eval_jaxpr/ppermute | solution.py:10
  130.2 9.1 %collective-permute-start = (bf16[32,4096]{1,0:T(8,128)(2,1)}, bf16[32,4096]{1,0:T(8,128)(2,1)S(1)}, u32[]{:S(2)}, u32[]{:S(2)}) collective-permute-start(bf16[32,4096]{1,0:T(8,128)(2,1)} %get-tuple-element.1282), channel_id=1, source_target_pairs={{32,0},{64,32},{96,64},{128,96},{160,128},{192,160},{224,192},{256... | collective-permute-start | bytes 786440 | tf_op jit(solution)/shard_map/while/body/eval_jaxpr/ppermute | solution.py:10
  140.8 9.4 %collective-permute-start = (bf16[32,4096]{1,0:T(8,128)(2,1)}, bf16[32,4096]{1,0:T(8,128)(2,1)S(1)}, u32[]{:S(2)}, u32[]{:S(2)}) collective-permute-start(bf16[32,4096]{1,0:T(8,128)(2,1)} %get-tuple-element.1282), channel_id=1, source_target_pairs={{32,0},{64,32},{96,64},{128,96},{160,128},{192,160},{224,192},{256... | collective-permute-start | bytes 786440 | tf_op jit(solution)/shard_map/while/body/eval_jaxpr/ppermute | solution.py:10
  151.7 9.7 %collective-permute-start = (bf16[32,4096]{1,0:T(8,128)(2,1)}, bf16[32,4096]{1,0:T(8,128)(2,1)S(1)}, u32[]{:S(2)}, u32[]{:S(2)}) collective-permute-start(bf16[32,4096]{1,0:T(8,128)(2,1)} %get-tuple-element.1282), channel_id=1, source_target_pairs={{32,0},{64,32},{96,64},{128,96},{160,128},{192,160},{224,192},{256... | collective-permute-start | bytes 786440 | tf_op jit(solution)/shard_map/while/body/eval_jaxpr/ppermute | solution.py:10
  162.9 9.7 %collective-permute-start = (bf16[32,4096]{1,0:T(8,128)(2,1)}, bf16[32,4096]{1,0:T(8,128)(2,1)S(1)}, u32[]{:S(2)}, u32[]{:S(2)}) collective-permute-start(bf16[32,4096]{1,0:T(8,128)(2,1)} %get-tuple-element.1282), channel_id=1, source_target_pairs={{32,0},{64,32},{96,64},{128,96},{160,128},{192,160},{224,192},{256... | collective-permute-start | bytes 786440 | tf_op jit(solution)/shard_map/while/body/eval_jaxpr/ppermute | solution.py:10
  174.0 9.8 %collective-permute-start = (bf16[32,4096]{1,0:T(8,128)(2,1)}, bf16[32,4096]{1,0:T(8,128)(2,1)S(1)}, u32[]{:S(2)}, u32[]{:S(2)}) collective-permute-start(bf16[32,4096]{1,0:T(8,128)(2,1)} %get-tuple-element.1282), channel_id=1, source_target_pairs={{32,0},{64,32},{96,64},{128,96},{160,128},{192,160},{224,192},{256... | collective-permute-start | bytes 786440 | tf_op jit(solution)/shard_map/while/body/eval_jaxpr/ppermute | solution.py:10
  185.3 9.5 %collective-permute-start = (bf16[32,4096]{1,0:T(8,128)(2,1)}, bf16[32,4096]{1,0:T(8,128)(2,1)S(1)}, u32[]{:S(2)}, u32[]{:S(2)}) collective-permute-start(bf16[32,4096]{1,0:T(8,128)(2,1)} %get-tuple-element.1282), channel_id=1, source_target_pairs={{32,0},{64,32},{96,64},{128,96},{160,128},{192,160},{224,192},{256... | collective-permute-start | bytes 786440 | tf_op jit(solution)/shard_map/while/body/eval_jaxpr/ppermute | solution.py:10
  196.3 10.8 %collective-permute-start = (bf16[32,4096]{1,0:T(8,128)(2,1)}, bf16[32,4096]{1,0:T(8,128)(2,1)S(1)}, u32[]{:S(2)}, u32[]{:S(2)}) collective-permute-start(bf16[32,4096]{1,0:T(8,128)(2,1)} %get-tuple-element.1282), channel_id=1, source_target_pairs={{32,0},{64,32},{96,64},{128,96},{160,128},{192,160},{224,192},{256... | collective-permute-start | bytes 786440 | tf_op jit(solution)/shard_map/while/body/eval_jaxpr/ppermute | solution.py:10
  208.7 12.2 %collective-permute-start = (bf16[32,4096]{1,0:T(8,128)(2,1)}, bf16[32,4096]{1,0:T(8,128)(2,1)S(1)}, u32[]{:S(2)}, u32[]{:S(2)}) collective-permute-start(bf16[32,4096]{1,0:T(8,128)(2,1)} %get-tuple-element.1282), channel_id=1, source_target_pairs={{32,0},{64,32},{96,64},{128,96},{160,128},{192,160},{224,192},{256... | collective-permute-start | bytes 786440 | tf_op jit(solution)/shard_map/while/body/eval_jaxpr/ppermute | solution.py:10
  222.3 13.5 %collective-permute-start = (bf16[32,4096]{1,0:T(8,128)(2,1)}, bf16[32,4096]{1,0:T(8,128)(2,1)S(1)}, u32[]{:S(2)}, u32[]{:S(2)}) collective-permute-start(bf16[32,4096]{1,0:T(8,128)(2,1)} %get-tuple-element.1282), channel_id=1, source_target_pairs={{32,0},{64,32},{96,64},{128,96},{160,128},{192,160},{224,192},{256... | collective-permute-start | bytes 786440 | tf_op jit(solution)/shard_map/while/body/eval_jaxpr/ppermute | solution.py:10
  237.3 10.5 %collective-permute-start = (bf16[32,4096]{1,0:T(8,128)(2,1)}, bf16[32,4096]{1,0:T(8,128)(2,1)S(1)}, u32[]{:S(2)}, u32[]{:S(2)}) collective-permute-start(bf16[32,4096]{1,0:T(8,128)(2,1)} %get-tuple-element.1282), channel_id=1, source_target_pairs={{32,0},{64,32},{96,64},{128,96},{160,128},{192,160},{224,192},{256... | collective-permute-start | bytes 786440 | tf_op jit(solution)/shard_map/while/body/eval_jaxpr/ppermute | solution.py:10
  249.4 160.0 %collective-permute-start = (bf16[32,4096]{1,0:T(8,128)(2,1)}, bf16[32,4096]{1,0:T(8,128)(2,1)S(1)}, u32[]{:S(2)}, u32[]{:S(2)}) collective-permute-start(bf16[32,4096]{1,0:T(8,128)(2,1)} %get-tuple-element.1282), channel_id=1, source_target_pairs={{32,0},{64,32},{96,64},{128,96},{160,128},{192,160},{224,192},{256... | collective-permute-start | bytes 786440 | tf_op jit(solution)/shard_map/while/body/eval_jaxpr/ppermute | solution.py:10
  423.7 12.2 %collective-permute-start = (bf16[32,4096]{1,0:T(8,128)(2,1)}, bf16[32,4096]{1,0:T(8,128)(2,1)S(1)}, u32[]{:S(2)}, u32[]{:S(2)}) collective-permute-start(bf16[32,4096]{1,0:T(8,128)(2,1)} %get-tuple-element.1282), channel_id=1, source_target_pairs={{32,0},{64,32},{96,64},{128,96},{160,128},{192,160},{224,192},{256... | collective-permute-start | bytes 786440 | tf_op jit(solution)/shard_map/while/body/eval_jaxpr/ppermute | solution.py:10
  439.3 7.4 copy-start.7
  450.2 12.1 %collective-permute-start = (bf16[32,4096]{1,0:T(8,128)(2,1)}, bf16[32,4096]{1,0:T(8,128)(2,1)S(1)}, u32[]{:S(2)}, u32[]{:S(2)}) collective-permute-start(bf16[32,4096]{1,0:T(8,128)(2,1)} %get-tuple-element.1282), channel_id=1, source_target_pairs={{32,0},{64,32},{96,64},{128,96},{160,128},{192,160},{224,192},{256... | collective-permute-start | bytes 786440 | tf_op jit(solution)/shard_map/while/body/eval_jaxpr/ppermute | solution.py:10
  476.6 12.3 %collective-permute-start = (bf16[32,4096]{1,0:T(8,128)(2,1)}, bf16[32,4096]{1,0:T(8,128)(2,1)S(1)}, u32[]{:S(2)}, u32[]{:S(2)}) collective-permute-start(bf16[32,4096]{1,0:T(8,128)(2,1)} %get-tuple-element.1282), channel_id=1, source_target_pairs={{32,0},{64,32},{96,64},{128,96},{160,128},{192,160},{224,192},{256... | collective-permute-start | bytes 786440 | tf_op jit(solution)/shard_map/while/body/eval_jaxpr/ppermute | solution.py:10
  503.3 11.9 %collective-permute-start = (bf16[32,4096]{1,0:T(8,128)(2,1)}, bf16[32,4096]{1,0:T(8,128)(2,1)S(1)}, u32[]{:S(2)}, u32[]{:S(2)}) collective-permute-start(bf16[32,4096]{1,0:T(8,128)(2,1)} %get-tuple-element.1282), channel_id=1, source_target_pairs={{32,0},{64,32},{96,64},{128,96},{160,128},{192,160},{224,192},{256... | collective-permute-start | bytes 786440 | tf_op jit(solution)/shard_map/while/body/eval_jaxpr/ppermute | solution.py:10
  518.7 7.4 copy-start.7
  529.5 12.2 %collective-permute-start = (bf16[32,4096]{1,0:T(8,128)(2,1)}, bf16[32,4096]{1,0:T(8,128)(2,1)S(1)}, u32[]{:S(2)}, u32[]{:S(2)}) collective-permute-start(bf16[32,4096]{1,0:T(8,128)(2,1)} %get-tuple-element.1282), channel_id=1, source_target_pairs={{32,0},{64,32},{96,64},{128,96},{160,128},{192,160},{224,192},{256... | collective-permute-start | bytes 786440 | tf_op jit(solution)/shard_map/while/body/eval_jaxpr/ppermute | solution.py:10
  545.2 7.4 copy-start.7
  556.1 12.0 %collective-permute-start = (bf16[32,4096]{1,0:T(8,128)(2,1)}, bf16[32,4096]{1,0:T(8,128)(2,1)S(1)}, u32[]{:S(2)}, u32[]{:S(2)}) collective-permute-start(bf16[32,4096]{1,0:T(8,128)(2,1)} %get-tuple-element.1282), channel_id=1, source_target_pairs={{32,0},{64,32},{96,64},{128,96},{160,128},{192,160},{224,192},{256... | collective-permute-start | bytes 786440 | tf_op jit(solution)/shard_map/while/body/eval_jaxpr/ppermute | solution.py:10
  571.5 7.4 copy-start.7
  582.4 12.2 %collective-permute-start = (bf16[32,4096]{1,0:T(8,128)(2,1)}, bf16[32,4096]{1,0:T(8,128)(2,1)S(1)}, u32[]{:S(2)}, u32[]{:S(2)}) collective-permute-start(bf16[32,4096]{1,0:T(8,128)(2,1)} %get-tuple-element.1282), channel_id=1, source_target_pairs={{32,0},{64,32},{96,64},{128,96},{160,128},{192,160},{224,192},{256... | collective-permute-start | bytes 786440 | tf_op jit(solution)/shard_map/while/body/eval_jaxpr/ppermute | solution.py:10
  598.1 7.4 copy-start.7
  608.9 8.5 %collective-permute-start = (bf16[32,4096]{1,0:T(8,128)(2,1)}, bf16[32,4096]{1,0:T(8,128)(2,1)S(1)}, u32[]{:S(2)}, u32[]{:S(2)}) collective-permute-start(bf16[32,4096]{1,0:T(8,128)(2,1)} %get-tuple-element.1282), channel_id=1, source_target_pairs={{32,0},{64,32},{96,64},{128,96},{160,128},{192,160},{224,192},{256... | collective-permute-start | bytes 786440 | tf_op jit(solution)/shard_map/while/body/eval_jaxpr/ppermute | solution.py:10
  (27 other events, 43.8 us)
Sparse Core Ops, SparseCore 0:
  10.2 74.7 all-gather.3
  631.1 129.9 reduce-scatter.3
where the time goes:
time: 774 us; the launch traced here: 770 us
  waiting for transfers between devices  399 us (52%)
  blocking collectives  145 us (19%)
  matrix products  77.3 us (10%)
  local copies, waits for them, and re-layouts  47.5 us (6%)
  starting transfers between devices  44 us (6%)
  other arithmetic  41.4 us (5%)
  between operations  14.2 us (2%)
    ppermute x22, waiting for transfers between devices, passed_along(): lax.ppermute(value, axis, [(source, source + steps) for source in range(l...  343 us
    psum x1, blocking collectives, on_device(): gain_sum = lax.psum(gain_acc, 'fsdp')  104 us
    ppermute x22, starting transfers between devices, passed_along(): lax.ppermute(value, axis, [(source, source + steps) for source in range(l...  44 us
    all_gather x1, blocking collectives, on_device(): lax.all_gather(gain[0], 'fsdp', axis=0, tiled=True)  40.3 us
    dot_general x24, matrix products, contract_cols(): lax.dot_general(left, right, (((1,), (1,)), ((), ())), preferred_element_...  31.5 us
    all_gather x1, waiting for transfers between devices, on_device(): lax.all_gather(weights[0], 'fsdp', axis=0, tiled=True)  29.3 us
    unnamed x3, waiting for transfers between devices  26.4 us
  transfers between devices with their start and end apart: 24, of which 24 were waited for; matrix products, arithmetic and copies ran while one was open for 1% of the time, Pallas kernels for 0%

commit v1 on v0

--- a/solution.py
+++ b/solution.py
@@ -49,6 +49,19 @@
 
 
 def on_device(inputs, upstream, weights, gain):
+
+    def _drive_blocks(mine, ax_name, join_dim):
+        block_now = jnp.concatenate(
+            jax.lax.all_to_all(
+                jnp.stack([mine] * jax.lax.axis_size(ax_name), axis=0),
+                concat_axis=0,
+                axis_name=ax_name,
+                split_axis=0,
+            ),
+            axis=join_dim,
+        )
+        return block_now
+
     sections = lax.axis_size("section")
     here = lax.axis_index("section")
     micro_count = inputs.shape[1]
@@ -61,7 +74,7 @@
     normed = xfloat * inv_rms
     w_full, gain_full = (
         lax.all_gather(weights[0], "fsdp", axis=0, tiled=True),
-        lax.all_gather(gain[0], "fsdp", axis=0, tiled=True),
+        _drive_blocks(gain[0], "fsdp", 0),
     )
     hidden = (normed * gain_full.astype(jnp.float32)).astype(jnp.bfloat16)
     proj = jnp.dot(hidden, w_full[:, : 3 * head], preferred_element_type=jnp.float32)

time: 774 us -> 774 us (level)
  blocking collectives: 145 us -> 105 us
  waiting for transfers between devices: 399 us -> 427 us
  starting transfers between devices: 44 us -> 55.3 us
    all_gather x1 -> x0, blocking collectives: 40.3 us -> none  [on_device(): lax.all_gather(gain[0], 'fsdp', axis=0, tiled=True)]
    all_gather x1, waiting for transfers between devices: 29.3 us -> 53.9 us  [on_device(): lax.all_gather(weights[0], 'fsdp', axis=0, tiled=True)]
    all_to_all x0 -> x1, starting transfers between devices: none -> 11.6 us  [_drive_blocks(): jax.lax.all_to_all(jnp.stack([mine] * jax.lax.axis_size(ax_name), axis=0)...]
  transfers between devices with their start and end apart: 24 -> 25, of which waited for: 24 -> 25; matrix products, arithmetic and copies ran while one was open for 1% -> 1% of each run, Pallas kernels for 0% -> 0%
where the time goes in v1:
time: 774 us; the launch traced here: 770 us
  waiting for transfers between devices  427 us (55%)
  blocking collectives  105 us (14%)
  matrix products  77.3 us (10%)
  starting transfers between devices  55.3 us (7%)
  local copies, waits for them, and re-layouts  48.9 us (6%)
  other arithmetic  41.4 us (5%)
  between operations  14.2 us (2%)
    ppermute x22, waiting for transfers between devices, passed_along(): lax.ppermute(value, axis, [(source, source + steps) for source in range(l...  344 us
    psum x1, blocking collectives, on_device(): gain_sum = lax.psum(gain_acc, 'fsdp')  105 us
    all_gather x1, waiting for transfers between devices, on_device(): lax.all_gather(weights[0], 'fsdp', axis=0, tiled=True)  53.9 us
    ppermute x22, starting transfers between devices, passed_along(): lax.ppermute(value, axis, [(source, source + steps) for source in range(l...  43.6 us
    dot_general x24, matrix products, contract_cols(): lax.dot_general(left, right, (((1,), (1,)), ((), ())), preferred_element_...  31.5 us
    unnamed x3, waiting for transfers between devices  26.4 us
  transfers between devices with their start and end apart: 25, of which 25 were waited for; matrix products, arithmetic and copies ran while one was open for 1% of the time, Pallas kernels for 0%

profile of v1, /device:TPU:8, one launch (start us, length us, event | category | flops | bytes accessed | tf_op | source)
XLA Modules:
  0.0 770.1 jit_solution(1975130266579173879)
XLA Ops:
  9.2 11.6 %all-to-all-start = ((bf16[32,1,128]{2,1,0:T(2,128)(2,1)}), bf16[32,1,128]{2,1,0:T(2,128)(2,1)S(1)}, u32[]{:S(2)}, u32[]{:S(2)}) async-start(bf16[32,1,128]{2,1,0:T(2,128)(2,1)} %stack.3), calls=%async_computation | async-start | bytes 32768 | tf_op jit(solution)/shard_map/all_to_all | solution.py:55
  31.2 53.9 %all-gather.3.cloned.1.call-done = bf16[1,4096,512]{2,1,0:T(8,128)(2,1)} async-done(((bf16[1,128,512]{2,1,0:T(8,128)(2,1)}), bf16[1,4096,512]{2,1,0:T(8,128)(2,1)}) %all-gather.3.cloned.1.call-update) | async-done | bytes 4194320 | tf_op jit(solution)/shard_map/all_gather | solution.py:76
  95.0 523.2 %while.26 = (s32[]{:T(128)}, bf16[32,4096]{1,0:T(8,128)(2,1)}, bf16[8,32,4096]{2,1,0:T(8,128)(2,1)}, bf16[8,32,384]{2,1,0:T(8,128)(2,1)}, bf16[8,32,128]{2,1,0:T...) while((s32[]{:T(128)}, bf16[32,4096]{1,0:T(8,128)(2,1)}, ...), condition=%wide.region_9.10_spmd.clone.clone.clone, body=%wide.region_1.9_spmd.clone.clone.clone.sunk | while | flops 137564064 | bytes 10755985 | solution.py:165
  98.3 8.1 %collective-permute-done = bf16[32,4096]{1,0:T(8,128)(2,1)S(1)} collective-permute-done((bf16[32,4096]{1,0:T(8,128)(2,1)}, bf16[32,4096]{1,0:T(8,128)(2,1)S(1)}, u32[]{:S(2)}, u32[]{:S(2)}) %collective-permute-start) | collective-permute-done | bytes 262176 | tf_op jit(solution)/shard_map/while/body/eval_jaxpr/ppermute | solution.py:10
  121.5 7.4 collective-permute-done
  142.8 7.5 collective-permute-done
  153.7 7.8 %collective-permute-done = bf16[32,4096]{1,0:T(8,128)(2,1)S(1)} collective-permute-done((bf16[32,4096]{1,0:T(8,128)(2,1)}, bf16[32,4096]{1,0:T(8,128)(2,1)S(1)}, u32[]{:S(2)}, u32[]{:S(2)}) %collective-permute-start) | collective-permute-done | bytes 262176 | tf_op jit(solution)/shard_map/while/body/eval_jaxpr/ppermute | solution.py:10
  164.9 7.8 %collective-permute-done = bf16[32,4096]{1,0:T(8,128)(2,1)S(1)} collective-permute-done((bf16[32,4096]{1,0:T(8,128)(2,1)}, bf16[32,4096]{1,0:T(8,128)(2,1)S(1)}, u32[]{:S(2)}, u32[]{:S(2)}) %collective-permute-start) | collective-permute-done | bytes 262176 | tf_op jit(solution)/shard_map/while/body/eval_jaxpr/ppermute | solution.py:10
  176.0 7.9 %collective-permute-done = bf16[32,4096]{1,0:T(8,128)(2,1)S(1)} collective-permute-done((bf16[32,4096]{1,0:T(8,128)(2,1)}, bf16[32,4096]{1,0:T(8,128)(2,1)S(1)}, u32[]{:S(2)}, u32[]{:S(2)}) %collective-permute-start) | collective-permute-done | bytes 262176 | tf_op jit(solution)/shard_map/while/body/eval_jaxpr/ppermute | solution.py:10
  187.4 7.6 collective-permute-done
  198.4 8.9 %collective-permute-done = bf16[32,4096]{1,0:T(8,128)(2,1)S(1)} collective-permute-done((bf16[32,4096]{1,0:T(8,128)(2,1)}, bf16[32,4096]{1,0:T(8,128)(2,1)S(1)}, u32[]{:S(2)}, u32[]{:S(2)}) %collective-permute-start) | collective-permute-done | bytes 262176 | tf_op jit(solution)/shard_map/while/body/eval_jaxpr/ppermute | solution.py:10
  210.7 10.3 %collective-permute-done = bf16[32,4096]{1,0:T(8,128)(2,1)S(1)} collective-permute-done((bf16[32,4096]{1,0:T(8,128)(2,1)}, bf16[32,4096]{1,0:T(8,128)(2,1)S(1)}, u32[]{:S(2)}, u32[]{:S(2)}) %collective-permute-start) | collective-permute-done | bytes 262176 | tf_op jit(solution)/shard_map/while/body/eval_jaxpr/ppermute | solution.py:10
  224.4 11.6 %collective-permute-done = bf16[32,4096]{1,0:T(8,128)(2,1)S(1)} collective-permute-done((bf16[32,4096]{1,0:T(8,128)(2,1)}, bf16[32,4096]{1,0:T(8,128)(2,1)S(1)}, u32[]{:S(2)}, u32[]{:S(2)}) %collective-permute-start) | collective-permute-done | bytes 262176 | tf_op jit(solution)/shard_map/while/body/eval_jaxpr/ppermute | solution.py:10
  239.4 8.6 %collective-permute-done = bf16[32,4096]{1,0:T(8,128)(2,1)S(1)} collective-permute-done((bf16[32,4096]{1,0:T(8,128)(2,1)}, bf16[32,4096]{1,0:T(8,128)(2,1)S(1)}, u32[]{:S(2)}, u32[]{:S(2)}) %collective-permute-start) | collective-permute-done | bytes 262176 | tf_op jit(solution)/shard_map/while/body/eval_jaxpr/ppermute | solution.py:10
  251.4 158.1 %collective-permute-done = bf16[32,4096]{1,0:T(8,128)(2,1)S(1)} collective-permute-done((bf16[32,4096]{1,0:T(8,128)(2,1)}, bf16[32,4096]{1,0:T(8,128)(2,1)S(1)}, u32[]{:S(2)}, u32[]{:S(2)}) %collective-permute-start) | collective-permute-done | bytes 262176 | tf_op jit(solution)/shard_map/while/body/eval_jaxpr/ppermute | solution.py:10
  410.3 13.6 %conditional.7 = (bf16[32,4096]{1,0:T(8,128)(2,1)}, bf16[8,32,4096]{2,1,0:T(8,128)(2,1)}, bf16[8,32,384]{2,1,0:T(8,128)(2,1)}, bf16[8,32,128]{2,1,0:T(8,128)(2,1)}, f32[4096]{0:T(1024)S(1)}) conditional(s32[]{:T(128)} %convert_element_type.197, (bf16[8,32,4096]{2,1,0:T(8,128)(2,1)}, bf16[8,32,384]{2,1,0:T(8,128)(2,1)}, ...), branch_computations={%region_2.2_spmd, %region_3.8_spmd.clone} | conditional | flops 137562016 | bytes 8641706 | solution.py:148
  425.8 10.3 %collective-permute-done = bf16[32,4096]{1,0:T(8,128)(2,1)S(1)} collective-permute-done((bf16[32,4096]{1,0:T(8,128)(2,1)}, bf16[32,4096]{1,0:T(8,128)(2,1)S(1)}, u32[]{:S(2)}, u32[]{:S(2)}) %collective-permute-start) | collective-permute-done | bytes 262176 | tf_op jit(solution)/shard_map/while/body/eval_jaxpr/ppermute | solution.py:10
  436.8 13.6 %conditional.7 = (bf16[32,4096]{1,0:T(8,128)(2,1)}, bf16[8,32,4096]{2,1,0:T(8,128)(2,1)}, bf16[8,32,384]{2,1,0:T(8,128)(2,1)}, bf16[8,32,128]{2,1,0:T(8,128)(2,1)}, f32[4096]{0:T(1024)S(1)}) conditional(s32[]{:T(128)} %convert_element_type.197, (bf16[8,32,4096]{2,1,0:T(8,128)(2,1)}, bf16[8,32,384]{2,1,0:T(8,128)(2,1)}, ...), branch_computations={%region_2.2_spmd, %region_3.8_spmd.clone} | conditional | flops 137562016 | bytes 8641706 | solution.py:148
  452.3 10.2 %collective-permute-done = bf16[32,4096]{1,0:T(8,128)(2,1)S(1)} collective-permute-done((bf16[32,4096]{1,0:T(8,128)(2,1)}, bf16[32,4096]{1,0:T(8,128)(2,1)S(1)}, u32[]{:S(2)}, u32[]{:S(2)}) %collective-permute-start) | collective-permute-done | bytes 262176 | tf_op jit(solution)/shard_map/while/body/eval_jaxpr/ppermute | solution.py:10
  463.2 13.6 %conditional.7 = (bf16[32,4096]{1,0:T(8,128)(2,1)}, bf16[8,32,4096]{2,1,0:T(8,128)(2,1)}, bf16[8,32,384]{2,1,0:T(8,128)(2,1)}, bf16[8,32,128]{2,1,0:T(8,128)(2,1)}, f32[4096]{0:T(1024)S(1)}) conditional(s32[]{:T(128)} %convert_element_type.197, (bf16[8,32,4096]{2,1,0:T(8,128)(2,1)}, bf16[8,32,384]{2,1,0:T(8,128)(2,1)}, ...), branch_computations={%region_2.2_spmd, %region_3.8_spmd.clone} | conditional | flops 137562016 | bytes 8641706 | solution.py:148
  478.7 10.4 %collective-permute-done = bf16[32,4096]{1,0:T(8,128)(2,1)S(1)} collective-permute-done((bf16[32,4096]{1,0:T(8,128)(2,1)}, bf16[32,4096]{1,0:T(8,128)(2,1)S(1)}, u32[]{:S(2)}, u32[]{:S(2)}) %collective-permute-start) | collective-permute-done | bytes 262176 | tf_op jit(solution)/shard_map/while/body/eval_jaxpr/ppermute | solution.py:10
  489.8 13.6 %conditional.7 = (bf16[32,4096]{1,0:T(8,128)(2,1)}, bf16[8,32,4096]{2,1,0:T(8,128)(2,1)}, bf16[8,32,384]{2,1,0:T(8,128)(2,1)}, bf16[8,32,128]{2,1,0:T(8,128)(2,1)}, f32[4096]{0:T(1024)S(1)}) conditional(s32[]{:T(128)} %convert_element_type.197, (bf16[8,32,4096]{2,1,0:T(8,128)(2,1)}, bf16[8,32,384]{2,1,0:T(8,128)(2,1)}, ...), branch_computations={%region_2.2_spmd, %region_3.8_spmd.clone} | conditional | flops 137562016 | bytes 8641706 | solution.py:148
  505.4 10.0 %collective-permute-done = bf16[32,4096]{1,0:T(8,128)(2,1)S(1)} collective-permute-done((bf16[32,4096]{1,0:T(8,128)(2,1)}, bf16[32,4096]{1,0:T(8,128)(2,1)S(1)}, u32[]{:S(2)}, u32[]{:S(2)}) %collective-permute-start) | collective-permute-done | bytes 262176 | tf_op jit(solution)/shard_map/while/body/eval_jaxpr/ppermute | solution.py:10
  516.1 13.6 %conditional.7 = (bf16[32,4096]{1,0:T(8,128)(2,1)}, bf16[8,32,4096]{2,1,0:T(8,128)(2,1)}, bf16[8,32,384]{2,1,0:T(8,128)(2,1)}, bf16[8,32,128]{2,1,0:T(8,128)(2,1)}, f32[4096]{0:T(1024)S(1)}) conditional(s32[]{:T(128)} %convert_element_type.197, (bf16[8,32,4096]{2,1,0:T(8,128)(2,1)}, bf16[8,32,384]{2,1,0:T(8,128)(2,1)}, ...), branch_computations={%region_2.2_spmd, %region_3.8_spmd.clone} | conditional | flops 137562016 | bytes 8641706 | solution.py:148
  531.6 10.2 %collective-permute-done = bf16[32,4096]{1,0:T(8,128)(2,1)S(1)} collective-permute-done((bf16[32,4096]{1,0:T(8,128)(2,1)}, bf16[32,4096]{1,0:T(8,128)(2,1)S(1)}, u32[]{:S(2)}, u32[]{:S(2)}) %collective-permute-start) | collective-permute-done | bytes 262176 | tf_op jit(solution)/shard_map/while/body/eval_jaxpr/ppermute | solution.py:10
  542.6 13.6 %conditional.7 = (bf16[32,4096]{1,0:T(8,128)(2,1)}, bf16[8,32,4096]{2,1,0:T(8,128)(2,1)}, bf16[8,32,384]{2,1,0:T(8,128)(2,1)}, bf16[8,32,128]{2,1,0:T(8,128)(2,1)}, f32[4096]{0:T(1024)S(1)}) conditional(s32[]{:T(128)} %convert_element_type.197, (bf16[8,32,4096]{2,1,0:T(8,128)(2,1)}, bf16[8,32,384]{2,1,0:T(8,128)(2,1)}, ...), branch_computations={%region_2.2_spmd, %region_3.8_spmd.clone} | conditional | flops 137562016 | bytes 8641706 | solution.py:148
  558.2 10.1 %collective-permute-done = bf16[32,4096]{1,0:T(8,128)(2,1)S(1)} collective-permute-done((bf16[32,4096]{1,0:T(8,128)(2,1)}, bf16[32,4096]{1,0:T(8,128)(2,1)S(1)}, u32[]{:S(2)}, u32[]{:S(2)}) %collective-permute-start) | collective-permute-done | bytes 262176 | tf_op jit(solution)/shard_map/while/body/eval_jaxpr/ppermute | solution.py:10
  569.0 13.6 %conditional.7 = (bf16[32,4096]{1,0:T(8,128)(2,1)}, bf16[8,32,4096]{2,1,0:T(8,128)(2,1)}, bf16[8,32,384]{2,1,0:T(8,128)(2,1)}, bf16[8,32,128]{2,1,0:T(8,128)(2,1)}, f32[4096]{0:T(1024)S(1)}) conditional(s32[]{:T(128)} %convert_element_type.197, (bf16[8,32,4096]{2,1,0:T(8,128)(2,1)}, bf16[8,32,384]{2,1,0:T(8,128)(2,1)}, ...), branch_computations={%region_2.2_spmd, %region_3.8_spmd.clone} | conditional | flops 137562016 | bytes 8641706 | solution.py:148
  584.5 10.2 %collective-permute-done = bf16[32,4096]{1,0:T(8,128)(2,1)S(1)} collective-permute-done((bf16[32,4096]{1,0:T(8,128)(2,1)}, bf16[32,4096]{1,0:T(8,128)(2,1)S(1)}, u32[]{:S(2)}, u32[]{:S(2)}) %collective-permute-start) | collective-permute-done | bytes 262176 | tf_op jit(solution)/shard_map/while/body/eval_jaxpr/ppermute | solution.py:10
  595.5 13.6 %conditional.7 = (bf16[32,4096]{1,0:T(8,128)(2,1)}, bf16[8,32,4096]{2,1,0:T(8,128)(2,1)}, bf16[8,32,384]{2,1,0:T(8,128)(2,1)}, bf16[8,32,128]{2,1,0:T(8,128)(2,1)}, f32[4096]{0:T(1024)S(1)}) conditional(s32[]{:T(128)} %convert_element_type.197, (bf16[8,32,4096]{2,1,0:T(8,128)(2,1)}, bf16[8,32,384]{2,1,0:T(8,128)(2,1)}, ...), branch_computations={%region_2.2_spmd, %region_3.8_spmd.clone} | conditional | flops 137562016 | bytes 8641706 | solution.py:148
  631.1 104.5 %psum.7 = f32[1,4096]{1,0:T(1,128)} all-reduce(f32[1,4096]{1,0:T(1,128)S(1)} %bitcast.143), channel_id=1, replica_groups=mesh['section'=16,'fsdp'=32] {'fsdp'}, use_global_device_ids=true, to_apply=%region_17.18 | all-reduce | flops 4096 | bytes 32768 | tf_op jit(solution)/shard_map/psum | solution.py:170
  735.6 25.7 %reduce-scatter.4.cloned.1.call-done = bf16[128,512]{1,0:T(8,128)(2,1)} async-done(((bf16[4096,512]{1,0:T(8,128)(2,1)}), bf16[128,512]{1,0:T(8,128)(2,1)}) %reduce-scatter.4.cloned.1.call-update) | async-done | bytes 131088
  (377 shorter events, 246.0 us)
Async XLA Ops:
  7.2 15.9 %copy-start = (bf16[1,8,32,4096]{3,2,1,0:T(8,128)(2,1)S(1)}, bf16[1,8,32,4096]{3,2,1,0:T(8,128)(2,1)}, u32[]{:S(2)}) copy-start(bf16[1,8,32,4096]{3,2,1,0:T(8,128)(2,1)} %param.10) | copy-start | bytes 6291460
  7.2 77.9 %all-gather.3.cloned.1.call-start = ((), (), s32[]{:S(2)}) async-start(), calls=%async_computation.2 | async-start | bytes 4325376 | tf_op jit(solution)/shard_map/all_gather | solution.py:76
  9.2 20.0 %all-to-all-start = ((bf16[32,1,128]{2,1,0:T(2,128)(2,1)}), bf16[32,1,128]{2,1,0:T(2,128)(2,1)S(1)}, u32[]{:S(2)}, u32[]{:S(2)}) async-start(bf16[32,1,128]{2,1,0:T(2,128)(2,1)} %stack.3), calls=%async_computation | async-start | bytes 32768 | tf_op jit(solution)/shard_map/all_to_all | solution.py:55
  20.8 740.5 %reduce-scatter.4.cloned.1.call-start = ((), (), s32[]{:S(2)}) async-start(), calls=%async_computation.3 | async-start | bytes 4325376
  25.6 64.9 %copy-start.5 = (f32[32,64]{1,0:T(8,128)}, f32[32,64]{1,0:T(8,128)S(1)}, u32[]{:S(2)}) copy-start(f32[32,64]{1,0:T(8,128)S(1)} %get-tuple-element.1389) | copy-start | bytes 24580
  25.6 64.9 %copy-start.6 = (f32[32,64]{1,0:T(8,128)}, f32[32,64]{1,0:T(8,128)S(1)}, u32[]{:S(2)}) copy-start(f32[32,64]{1,0:T(8,128)S(1)} %get-tuple-element.1390) | copy-start | bytes 24580
  95.8 10.5 %collective-permute-start = (bf16[32,4096]{1,0:T(8,128)(2,1)}, bf16[32,4096]{1,0:T(8,128)(2,1)S(1)}, u32[]{:S(2)}, u32[]{:S(2)}) collective-permute-start(bf16[32,4096]{1,0:T(8,128)(2,1)} %get-tuple-element.1282), channel_id=1, source_target_pairs={{32,0},{64,32},{96,64},{128,96},{160,128},{192,160},{224,192},{256... | collective-permute-start | bytes 786440 | tf_op jit(solution)/shard_map/while/body/eval_jaxpr/ppermute | solution.py:10
  107.8 9.7 %collective-permute-start = (bf16[32,4096]{1,0:T(8,128)(2,1)}, bf16[32,4096]{1,0:T(8,128)(2,1)S(1)}, u32[]{:S(2)}, u32[]{:S(2)}) collective-permute-start(bf16[32,4096]{1,0:T(8,128)(2,1)} %get-tuple-element.1282), channel_id=1, source_target_pairs={{32,0},{64,32},{96,64},{128,96},{160,128},{192,160},{224,192},{256... | collective-permute-start | bytes 786440 | tf_op jit(solution)/shard_map/while/body/eval_jaxpr/ppermute | solution.py:10
  119.0 9.8 %collective-permute-start = (bf16[32,4096]{1,0:T(8,128)(2,1)}, bf16[32,4096]{1,0:T(8,128)(2,1)S(1)}, u32[]{:S(2)}, u32[]{:S(2)}) collective-permute-start(bf16[32,4096]{1,0:T(8,128)(2,1)} %get-tuple-element.1282), channel_id=1, source_target_pairs={{32,0},{64,32},{96,64},{128,96},{160,128},{192,160},{224,192},{256... | collective-permute-start | bytes 786440 | tf_op jit(solution)/shard_map/while/body/eval_jaxpr/ppermute | solution.py:10
  130.3 9.1 %collective-permute-start = (bf16[32,4096]{1,0:T(8,128)(2,1)}, bf16[32,4096]{1,0:T(8,128)(2,1)S(1)}, u32[]{:S(2)}, u32[]{:S(2)}) collective-permute-start(bf16[32,4096]{1,0:T(8,128)(2,1)} %get-tuple-element.1282), channel_id=1, source_target_pairs={{32,0},{64,32},{96,64},{128,96},{160,128},{192,160},{224,192},{256... | collective-permute-start | bytes 786440 | tf_op jit(solution)/shard_map/while/body/eval_jaxpr/ppermute | solution.py:10
  140.9 9.4 %collective-permute-start = (bf16[32,4096]{1,0:T(8,128)(2,1)}, bf16[32,4096]{1,0:T(8,128)(2,1)S(1)}, u32[]{:S(2)}, u32[]{:S(2)}) collective-permute-start(bf16[32,4096]{1,0:T(8,128)(2,1)} %get-tuple-element.1282), channel_id=1, source_target_pairs={{32,0},{64,32},{96,64},{128,96},{160,128},{192,160},{224,192},{256... | collective-permute-start | bytes 786440 | tf_op jit(solution)/shard_map/while/body/eval_jaxpr/ppermute | solution.py:10
  151.8 9.7 %collective-permute-start = (bf16[32,4096]{1,0:T(8,128)(2,1)}, bf16[32,4096]{1,0:T(8,128)(2,1)S(1)}, u32[]{:S(2)}, u32[]{:S(2)}) collective-permute-start(bf16[32,4096]{1,0:T(8,128)(2,1)} %get-tuple-element.1282), channel_id=1, source_target_pairs={{32,0},{64,32},{96,64},{128,96},{160,128},{192,160},{224,192},{256... | collective-permute-start | bytes 786440 | tf_op jit(solution)/shard_map/while/body/eval_jaxpr/ppermute | solution.py:10
  163.0 9.7 %collective-permute-start = (bf16[32,4096]{1,0:T(8,128)(2,1)}, bf16[32,4096]{1,0:T(8,128)(2,1)S(1)}, u32[]{:S(2)}, u32[]{:S(2)}) collective-permute-start(bf16[32,4096]{1,0:T(8,128)(2,1)} %get-tuple-element.1282), channel_id=1, source_target_pairs={{32,0},{64,32},{96,64},{128,96},{160,128},{192,160},{224,192},{256... | collective-permute-start | bytes 786440 | tf_op jit(solution)/shard_map/while/body/eval_jaxpr/ppermute | solution.py:10
  174.1 9.8 %collective-permute-start = (bf16[32,4096]{1,0:T(8,128)(2,1)}, bf16[32,4096]{1,0:T(8,128)(2,1)S(1)}, u32[]{:S(2)}, u32[]{:S(2)}) collective-permute-start(bf16[32,4096]{1,0:T(8,128)(2,1)} %get-tuple-element.1282), channel_id=1, source_target_pairs={{32,0},{64,32},{96,64},{128,96},{160,128},{192,160},{224,192},{256... | collective-permute-start | bytes 786440 | tf_op jit(solution)/shard_map/while/body/eval_jaxpr/ppermute | solution.py:10
  185.5 9.5 %collective-permute-start = (bf16[32,4096]{1,0:T(8,128)(2,1)}, bf16[32,4096]{1,0:T(8,128)(2,1)S(1)}, u32[]{:S(2)}, u32[]{:S(2)}) collective-permute-start(bf16[32,4096]{1,0:T(8,128)(2,1)} %get-tuple-element.1282), channel_id=1, source_target_pairs={{32,0},{64,32},{96,64},{128,96},{160,128},{192,160},{224,192},{256... | collective-permute-start | bytes 786440 | tf_op jit(solution)/shard_map/while/body/eval_jaxpr/ppermute | solution.py:10
  196.4 10.8 %collective-permute-start = (bf16[32,4096]{1,0:T(8,128)(2,1)}, bf16[32,4096]{1,0:T(8,128)(2,1)S(1)}, u32[]{:S(2)}, u32[]{:S(2)}) collective-permute-start(bf16[32,4096]{1,0:T(8,128)(2,1)} %get-tuple-element.1282), channel_id=1, source_target_pairs={{32,0},{64,32},{96,64},{128,96},{160,128},{192,160},{224,192},{256... | collective-permute-start | bytes 786440 | tf_op jit(solution)/shard_map/while/body/eval_jaxpr/ppermute | solution.py:10
  208.8 12.2 %collective-permute-start = (bf16[32,4096]{1,0:T(8,128)(2,1)}, bf16[32,4096]{1,0:T(8,128)(2,1)S(1)}, u32[]{:S(2)}, u32[]{:S(2)}) collective-permute-start(bf16[32,4096]{1,0:T(8,128)(2,1)} %get-tuple-element.1282), channel_id=1, source_target_pairs={{32,0},{64,32},{96,64},{128,96},{160,128},{192,160},{224,192},{256... | collective-permute-start | bytes 786440 | tf_op jit(solution)/shard_map/while/body/eval_jaxpr/ppermute | solution.py:10
  222.4 13.5 %collective-permute-start = (bf16[32,4096]{1,0:T(8,128)(2,1)}, bf16[32,4096]{1,0:T(8,128)(2,1)S(1)}, u32[]{:S(2)}, u32[]{:S(2)}) collective-permute-start(bf16[32,4096]{1,0:T(8,128)(2,1)} %get-tuple-element.1282), channel_id=1, source_target_pairs={{32,0},{64,32},{96,64},{128,96},{160,128},{192,160},{224,192},{256... | collective-permute-start | bytes 786440 | tf_op jit(solution)/shard_map/while/body/eval_jaxpr/ppermute | solution.py:10
  237.5 10.5 %collective-permute-start = (bf16[32,4096]{1,0:T(8,128)(2,1)}, bf16[32,4096]{1,0:T(8,128)(2,1)S(1)}, u32[]{:S(2)}, u32[]{:S(2)}) collective-permute-start(bf16[32,4096]{1,0:T(8,128)(2,1)} %get-tuple-element.1282), channel_id=1, source_target_pairs={{32,0},{64,32},{96,64},{128,96},{160,128},{192,160},{224,192},{256... | collective-permute-start | bytes 786440 | tf_op jit(solution)/shard_map/while/body/eval_jaxpr/ppermute | solution.py:10
  249.5 160.0 %collective-permute-start = (bf16[32,4096]{1,0:T(8,128)(2,1)}, bf16[32,4096]{1,0:T(8,128)(2,1)S(1)}, u32[]{:S(2)}, u32[]{:S(2)}) collective-permute-start(bf16[32,4096]{1,0:T(8,128)(2,1)} %get-tuple-element.1282), channel_id=1, source_target_pairs={{32,0},{64,32},{96,64},{128,96},{160,128},{192,160},{224,192},{256... | collective-permute-start | bytes 786440 | tf_op jit(solution)/shard_map/while/body/eval_jaxpr/ppermute | solution.py:10
  423.8 12.2 %collective-permute-start = (bf16[32,4096]{1,0:T(8,128)(2,1)}, bf16[32,4096]{1,0:T(8,128)(2,1)S(1)}, u32[]{:S(2)}, u32[]{:S(2)}) collective-permute-start(bf16[32,4096]{1,0:T(8,128)(2,1)} %get-tuple-element.1282), channel_id=1, source_target_pairs={{32,0},{64,32},{96,64},{128,96},{160,128},{192,160},{224,192},{256... | collective-permute-start | bytes 786440 | tf_op jit(solution)/shard_map/while/body/eval_jaxpr/ppermute | solution.py:10
  439.5 7.4 copy-start.7
  450.4 12.1 %collective-permute-start = (bf16[32,4096]{1,0:T(8,128)(2,1)}, bf16[32,4096]{1,0:T(8,128)(2,1)S(1)}, u32[]{:S(2)}, u32[]{:S(2)}) collective-permute-start(bf16[32,4096]{1,0:T(8,128)(2,1)} %get-tuple-element.1282), channel_id=1, source_target_pairs={{32,0},{64,32},{96,64},{128,96},{160,128},{192,160},{224,192},{256... | collective-permute-start | bytes 786440 | tf_op jit(solution)/shard_map/while/body/eval_jaxpr/ppermute | solution.py:10
  476.8 12.3 %collective-permute-start = (bf16[32,4096]{1,0:T(8,128)(2,1)}, bf16[32,4096]{1,0:T(8,128)(2,1)S(1)}, u32[]{:S(2)}, u32[]{:S(2)}) collective-permute-start(bf16[32,4096]{1,0:T(8,128)(2,1)} %get-tuple-element.1282), channel_id=1, source_target_pairs={{32,0},{64,32},{96,64},{128,96},{160,128},{192,160},{224,192},{256... | collective-permute-start | bytes 786440 | tf_op jit(solution)/shard_map/while/body/eval_jaxpr/ppermute | solution.py:10
  503.5 11.9 %collective-permute-start = (bf16[32,4096]{1,0:T(8,128)(2,1)}, bf16[32,4096]{1,0:T(8,128)(2,1)S(1)}, u32[]{:S(2)}, u32[]{:S(2)}) collective-permute-start(bf16[32,4096]{1,0:T(8,128)(2,1)} %get-tuple-element.1282), channel_id=1, source_target_pairs={{32,0},{64,32},{96,64},{128,96},{160,128},{192,160},{224,192},{256... | collective-permute-start | bytes 786440 | tf_op jit(solution)/shard_map/while/body/eval_jaxpr/ppermute | solution.py:10
  529.7 12.2 %collective-permute-start = (bf16[32,4096]{1,0:T(8,128)(2,1)}, bf16[32,4096]{1,0:T(8,128)(2,1)S(1)}, u32[]{:S(2)}, u32[]{:S(2)}) collective-permute-start(bf16[32,4096]{1,0:T(8,128)(2,1)} %get-tuple-element.1282), channel_id=1, source_target_pairs={{32,0},{64,32},{96,64},{128,96},{160,128},{192,160},{224,192},{256... | collective-permute-start | bytes 786440 | tf_op jit(solution)/shard_map/while/body/eval_jaxpr/ppermute | solution.py:10
  545.4 7.4 copy-start.7
  556.3 12.0 %collective-permute-start = (bf16[32,4096]{1,0:T(8,128)(2,1)}, bf16[32,4096]{1,0:T(8,128)(2,1)S(1)}, u32[]{:S(2)}, u32[]{:S(2)}) collective-permute-start(bf16[32,4096]{1,0:T(8,128)(2,1)} %get-tuple-element.1282), channel_id=1, source_target_pairs={{32,0},{64,32},{96,64},{128,96},{160,128},{192,160},{224,192},{256... | collective-permute-start | bytes 786440 | tf_op jit(solution)/shard_map/while/body/eval_jaxpr/ppermute | solution.py:10
  571.7 7.4 copy-start.7
  582.6 12.2 %collective-permute-start = (bf16[32,4096]{1,0:T(8,128)(2,1)}, bf16[32,4096]{1,0:T(8,128)(2,1)S(1)}, u32[]{:S(2)}, u32[]{:S(2)}) collective-permute-start(bf16[32,4096]{1,0:T(8,128)(2,1)} %get-tuple-element.1282), channel_id=1, source_target_pairs={{32,0},{64,32},{96,64},{128,96},{160,128},{192,160},{224,192},{256... | collective-permute-start | bytes 786440 | tf_op jit(solution)/shard_map/while/body/eval_jaxpr/ppermute | solution.py:10
  598.2 7.4 copy-start.7
  609.1 8.5 %collective-permute-start = (bf16[32,4096]{1,0:T(8,128)(2,1)}, bf16[32,4096]{1,0:T(8,128)(2,1)S(1)}, u32[]{:S(2)}, u32[]{:S(2)}) collective-permute-start(bf16[32,4096]{1,0:T(8,128)(2,1)} %get-tuple-element.1282), channel_id=1, source_target_pairs={{32,0},{64,32},{96,64},{128,96},{160,128},{192,160},{224,192},{256... | collective-permute-start | bytes 786440 | tf_op jit(solution)/shard_map/while/body/eval_jaxpr/ppermute | solution.py:10
  (28 other events, 51.1 us)
Sparse Core Ops, SparseCore 0:
  10.2 74.8 all-gather.2
  631.3 130.0 reduce-scatter.3
